TPU v7x, 32 devices: a whole 2x2x4 slice. The times are simulated.
32 devices in a mesh: dp: 2 (over x), expert: 16 (over z, y, core).
Axes of the slice: x: 2, y: 2, z: 4, core: 2. Of those that a mesh axis runs over, the one named last changes fastest.
Arguments:
- tokens: bfloat16 [8192, 1024], P(('dp', 'expert')), may hold values from -6 to 6
- modulation: bfloat16 [32, 2, 1024], P(('dp', 'expert')), may hold values from -3 to 3
- router_weight: bfloat16 [1024, 16], replicated, may hold values from -0.1875 to 0.1875
- weight_in: bfloat16 [16, 1024, 4096], P('expert', None, 'dp'), may hold values from -0.1875 to 0.1875
- weight_out: bfloat16 [16, 4096, 1024], P('expert', 'dp'), may hold values from -0.09375 to 0.09375
- chosen: int32 [2, 16, 256], P('dp'), may hold values from 0 to 4095, as said below
- grad_out: bfloat16 [8192, 1024], P(('dp', 'expert')), may hold values from -4 to 4
Outputs:
- grad_tokens: bfloat16 [8192, 1024], P(('dp', 'expert'))
- grad_mod: float32 [32, 2, 1024], P(('dp', 'expert'))
- grad_router: float32 [1024, 16], replicated
- grad_weight_in: bfloat16 [16, 1024, 4096], P('expert', None, 'dp')
- grad_weight_out: bfloat16 [16, 4096, 1024], P('expert', 'dp')
Inputs may be any that keep to these rules, and one draw needn't show every extreme that they name: `chosen`: for each slice and expert the 256 positions are distinct; at most 32 of them lie in one image's 256 tokens, and in one image exactly 32.
All inputs are finite; a program needn't handle non-finite values.
Results may differ from a plain program's by a relative error of at most 0.008.
Values may be sent and summed in bfloat16 or wider, within the bound.
No kernel may reach another device: no remote copies, remote signals or barrier semaphores. Data moves between devices by JAX's collectives and lax.ppermute only.
A program may use at most 128 MiB of HBM per device.

v0:
```python
import functools

import jax
import jax.numpy as jnp
from jax import lax
from jax.experimental import pallas as pl
from jax.experimental.pallas import tpu as pltpu
from jax.sharding import PartitionSpec as P

gelu_root = 0.7978845608028654
gelu_cube = 0.044715
norm_eps = 1e-06
bf16, f32, i32 = jnp.bfloat16, jnp.float32, jnp.int32


def gelu_both(values):
    tangent = jnp.tanh(gelu_root * (values + gelu_cube * values * values * values))
    value = 0.5 * values * (1.0 + tangent)
    slope = 0.5 * (1.0 + tangent) + 0.5 * values * (1.0 - tangent * tangent) * gelu_root * (
        1.0 + 3.0 * gelu_cube * values * values
    )
    return value, slope


def contract(left, right, left_dim, right_dim):
    return lax.dot_general(
        left, right, (((left_dim,), (right_dim,)), ((), ())), preferred_element_type=f32
    )


def iota(shape, dim):
    return lax.broadcasted_iota(i32, shape, dim)


def normalise(tokens):
    x_float = tokens.astype(f32)
    centred = x_float - jnp.mean(x_float, axis=1, keepdims=True)
    spread = jnp.mean(centred * centred, axis=1, keepdims=True)
    inverse = lax.rsqrt(spread + norm_eps)
    return centred * inverse, inverse


def prep_u_kernel(me_ref, chosen_ref, tokens_ref, mod_ref, *outs):
    experts, cap = chosen_ref.shape
    tok_count = tokens_ref.shape[0]
    most = 2 * tok_count // experts
    *u_outs, select_ref, slot_ref = outs
    me = me_ref[0]

    lanes = max(128, experts)
    padded = chosen_ref[...]
    if lanes > experts:
        padded = jnp.concatenate([padded, jnp.zeros((lanes - experts, cap), i32)], axis=0)
    local = jnp.transpose(padded) - me * tok_count
    token_row = iota((cap, tok_count), 1)
    member = [
        jnp.sum((local[:, e : e + 1] == token_row).astype(f32), axis=0, keepdims=True)
        for e in range(experts)
    ]
    member = jnp.concatenate(member, axis=0)
    before = (iota((tok_count, tok_count), 0) < iota((tok_count, tok_count), 1)).astype(bf16)
    rank = contract(member.astype(bf16), before, 1, 0)
    slot = jnp.where(member > 0.5, rank.astype(i32), -1)
    slot_ref[...] = slot
    slot_id = iota((most, tok_count), 0)

    def one_hot(row):
        return (row == slot_id).astype(f32).astype(bf16)

    normed, _ = normalise(tokens_ref[...])
    mod = mod_ref[...].astype(f32)
    normal_u = (normed * (1.0 + mod[1:2]) + mod[0:1]).astype(bf16)
    crossed = jnp.concatenate(
        [one_hot(slot_ref[pl.ds(me ^ k, 1), :]) for k in range(experts)], axis=0
    )
    sent = contract(crossed, normal_u, 1, 0).astype(bf16)
    for k in range(experts):
        u_outs[k][...] = sent[k * most : (k + 1) * most]
    for e in range(experts):
        select_ref[e * most : (e + 1) * most, :] = one_hot(slot[e : e + 1])


def prep_g_kernel(most, me_ref, chosen_ref, select_ref, grad_ref, g_out, u_place, g_place, spread):
    _, cap = chosen_ref.shape
    slots, tok_count = select_ref.shape
    me = me_ref[0]
    g_out[...] = contract(select_ref[...], grad_ref[...], 1, 0).astype(bf16)

    row = chosen_ref[pl.ds(me, 1), :]
    mine = jnp.transpose(jnp.concatenate([row] * 128, axis=0))[:, 0:1]
    image = lax.shift_right_logical(mine, tok_count.bit_length() - 1)
    lane = iota((1, slots), 1)
    block = lax.shift_right_logical(lane, most.bit_length() - 1)
    offset = lane & (most - 1)

    def places(source):
        count = jnp.sum((image == source).astype(f32), axis=0, keepdims=True).astype(i32)
        start = jnp.sum((image < source).astype(f32), axis=0, keepdims=True).astype(i32)
        place = jnp.where(offset < count, start + offset, -1)
        return (iota((cap, slots), 0) == place).astype(f32)

    u_place[...] = places(block ^ me).astype(bf16)
    ordered = places(block)
    g_place[...] = ordered.astype(bf16)
    spread[...] = jnp.transpose(ordered).astype(bf16)


scalar_spec = pl.BlockSpec(memory_space=pltpu.SMEM)
big = pltpu.CompilerParams(vmem_limit_bytes=56 * 1024 * 1024)


def swap_dp(values):
    count = lax.axis_size("dp")
    return lax.ppermute(values, "dp", [(i, count - 1 - i) for i in range(count)])


def pairwise(blocks):
    count = len(blocks)
    got = {0: blocks[0]}
    for k in range(count - 1, 0, -1):
        got[k] = lax.ppermute(blocks[k], "expert", [(i, i ^ k) for i in range(count)])
    return jnp.concatenate([got[k] for k in range(count)], axis=0)


def exchange(rows, experts):
    blocks = rows.reshape(experts, -1, rows.shape[1])
    return lax.all_to_all(blocks, "expert", 0, 0, tiled=True).reshape(rows.shape)


def expert_rows(rows_u, rows_g, router_weight, router_col, me, first_w, second_w):
    probs = jax.nn.sigmoid(contract(rows_u, router_weight, 1, 0)).astype(bf16).astype(f32)
    gate = jnp.sum(jnp.where(iota(probs.shape, 1) == me, probs, 0.0), axis=1, keepdims=True)
    preact = contract(rows_u, first_w, 1, 0)
    value, slope = gelu_both(preact)
    hidden = value.astype(bf16)
    upstream = contract(rows_g, second_w, 1, 1)
    score_part = jnp.sum(hidden.astype(f32) * upstream, axis=1, keepdims=True)
    grad_y = (gate * rows_g.astype(f32)).astype(bf16)
    grad_pre = (gate * upstream * slope).astype(bf16)
    logit_part = score_part * gate * (1.0 - gate)
    rows_part = contract(grad_pre, first_w, 1, 1) + logit_part * router_col
    column = jnp.sum(rows_u.astype(f32) * logit_part, axis=0)
    return hidden, grad_y, grad_pre, rows_part, column


def body(tokens, modulation, router_weight, weight_in, weight_out, chosen, grad_out):
    tok_count, width = tokens.shape
    experts = lax.axis_size("expert")
    halves = lax.axis_size("dp")
    most = 2 * tok_count // experts
    cap = chosen.shape[2]
    me = lax.axis_index("expert").astype(i32)
    shape = jax.ShapeDtypeStruct
    slots = experts * most

    *u_blocks, select = pl.pallas_call(
        prep_u_kernel,
        in_specs=[scalar_spec] + [pl.BlockSpec()] * 3,
        out_shape=[shape((most, width), bf16)] * experts + [shape((slots, tok_count), bf16)],
        scratch_shapes=[pltpu.VMEM((experts, tok_count), i32)],
        compiler_params=big,
        name="prep_u",
    )(me.reshape(1), chosen[0], tokens, modulation[0])
    g_sent, u_place, g_place, spread = pl.pallas_call(
        functools.partial(prep_g_kernel, most),
        in_specs=[scalar_spec] + [pl.BlockSpec()] * 3,
        out_shape=[
            shape((slots, width), bf16),
            shape((cap, slots), bf16),
            shape((cap, slots), bf16),
            shape((slots, cap), bf16),
        ],
        compiler_params=big,
        name="prep_g",
    )(me.reshape(1), chosen[0], select, grad_out)

    g_got = exchange(g_sent, experts)
    u_own = contract(u_place, pairwise(u_blocks), 1, 0).astype(bf16)
    u_other = swap_dp(u_own)
    g_own = contract(g_place, g_got, 1, 0).astype(bf16)
    g_other = swap_dp(g_own)

    first_w, second_w = weight_in[0], weight_out[0]
    router_col = lax.dynamic_index_in_dim(router_weight, me, 1, keepdims=False).astype(f32)
    shared = (router_weight, router_col, me, first_w, second_w)
    hidden_own, y_own, pre_own, back_own, column_own = expert_rows(u_own, g_own, *shared)
    back_own, column_own, g_other = lax.optimization_barrier((back_own, column_own, g_other))
    hidden_other, y_other, pre_other, back_other, column_other = expert_rows(
        u_other, g_other, *shared
    )

    total = (back_own + swap_dp(back_other.astype(bf16)).astype(f32)).astype(bf16)
    returned = exchange(contract(spread, total, 1, 0).astype(bf16), experts)

    columns = lax.all_to_all(
        jnp.broadcast_to(column_own + column_other, (halves * experts, width)),
        ("dp", "expert"), 0, 0, tiled=True,
    )
    grad_router = jnp.sum(columns.reshape(halves, experts, width), axis=0).T

    rows_u = jnp.concatenate([u_own, u_other], axis=0)
    hidden = jnp.concatenate([hidden_own, hidden_other], axis=0)
    grad_pre = jnp.concatenate([pre_own, pre_other], axis=0)
    grad_y = jnp.concatenate([y_own, y_other], axis=0)
    grad_weight_in = contract(rows_u, grad_pre, 0, 0).astype(bf16)[None]
    grad_weight_out = contract(hidden, grad_y, 0, 0).astype(bf16)[None]

    grad_u = contract(select, returned, 0, 0)
    normed, inverse = normalise(tokens)
    scale_mod = modulation[0, 1].astype(f32)
    grad_shift = jnp.sum(grad_u, axis=0)
    grad_scale = jnp.sum(grad_u * normed, axis=0)
    grad_mod = jnp.stack([grad_shift, grad_scale], axis=0)[None]
    grad_norm = grad_u * (1.0 + scale_mod)
    centre_term = jnp.mean(grad_norm, axis=1, keepdims=True)
    slope_term = jnp.mean(grad_norm * normed, axis=1, keepdims=True)
    grad_tokens = (
        grad_out.astype(f32) + (grad_norm - centre_term - normed * slope_term) * inverse
    ).astype(bf16)
    return (grad_tokens, grad_mod, grad_router, grad_weight_in, grad_weight_out)


def solution(mesh):
    placed = (
        P(("dp", "expert"), None),
        P(("dp", "expert"), None, None),
        P(),
        P("expert", None, "dp"),
        P("expert", "dp", None),
        P("dp", None, None),
        P(("dp", "expert"), None),
    )
    return jax.shard_map(
        body,
        mesh=mesh,
        in_specs=placed,
        out_specs=(
            P(("dp", "expert"), None),
            P(("dp", "expert"), None, None),
            P(),
            P("expert", None, "dp"),
            P("expert", "dp", None),
        ),
        check_vma=False,
    )
```

profile of v0, /device:TPU:0, one launch (start us, length us, event | category | flops | bytes accessed | tf_op | source)
XLA Modules:
  0.0 149.5 jit_solution(16775860723453901449)
XLA Ops:
  0.6 3.7 %prep_u.1 = (bf16[32,1024]{1,0:T(8,128)(2,1)}, bf16[32,1024]{1,0:T(8,128)(2,1)}, bf16[32,1024]{1,0:T(8,128)(2,1)}, bf16[32,1024]{1,0:T(8,128)(2,1)}, bf16[32,102...) custom-call(s32[1]{0:T(128)} %bitcast.me_ref, ...), custom_call_target="tpu_custom_call" | custom-call | tf_op jit(solution)/shard_map/prep_u/pallas_call | solution.py:156
  5.0 2.6 %collective-permute-start.1 = (bf16[32,1024]{1,0:T(8,128)(2,1)}, bf16[32,1024]{1,0:T(8,128)(2,1)S(1)}, u32[]{:S(2)}, u32[]{:S(2)}) collective-permute-start(bf16[32,1024]{1,0:T(8,128)(2,1)} %get-tuple-element.34), channel_id=1, source_target_pairs={{0,2},{1,3},{2,0},{3,1},{4,6},{5,7},{6,4},{7,5},{8,10},{9,11},{10,... | collective-permute-start | bytes 196616 | tf_op jit(solution)/shard_map/ppermute | solution.py:121
  7.6 1.8 %collective-permute-start.3 = (bf16[32,1024]{1,0:T(8,128)(2,1)}, bf16[32,1024]{1,0:T(8,128)(2,1)S(1)}, u32[]{:S(2)}, u32[]{:S(2)}) collective-permute-start(bf16[32,1024]{1,0:T(8,128)(2,1)} %get-tuple-element.36), channel_id=1, source_target_pairs={{0,4},{1,5},{2,6},{3,7},{4,0},{5,1},{6,2},{7,3},{8,12},{9,13},{10,... | collective-permute-start | bytes 196616 | tf_op jit(solution)/shard_map/ppermute | solution.py:121
  9.4 3.0 %prep_g.1 = (bf16[512,1024]{1,0:T(8,128)(2,1)}, bf16[256,512]{1,0:T(8,128)(2,1)}, bf16[256,512]{1,0:T(8,128)(2,1)}, bf16[512,256]{1,0:T(8,128)(2,1)}) custom-call(s32[1]{0:T(128)} %bitcast.me_ref, s32[16,256]{1,0:T(8,128)} %bitcast.66, bf16[512,256]{1,0:T(8,128)(2,1)} %get-tuple-element.29.select_ref, bf16[256,1024]{1,0:T(8,128)(2,1)} %grad_ref.1), custom_call_target="tpu_custom_call" | custom-call | tf_op jit(solution)/shard_map/prep_g/pallas_call | solution.py:164
  12.4 6.2 %all-to-all-start = ((bf16[16,32,1024]{2,1,0:T(8,128)(2,1)}), bf16[16,32,1024]{2,1,0:T(8,128)(2,1)S(1)}, u32[]{:S(2)}, u32[]{:S(2)}) async-start(bf16[16,32,1024]{2,1,0:T(8,128)(2,1)} %bitcast.61), calls=%async_computation | async-start | bytes 2097152 | tf_op jit(solution)/shard_map/all_to_all | solution.py:127
  18.7 2.9 %collective-permute-start.5 = (bf16[32,1024]{1,0:T(8,128)(2,1)S(1)}, bf16[32,1024]{1,0:T(8,128)(2,1)S(1)}, u32[]{:S(2)}, u32[]{:S(2)}) collective-permute-start(bf16[32,1024]{1,0:T(8,128)(2,1)S(1)} %copy-done.24), channel_id=1, source_target_pairs={{0,6},{1,7},{2,4},{3,5},{4,2},{5,3},{6,0},{7,1},{8,14},{9,15},{10,... | collective-permute-start | bytes 196616 | tf_op jit(solution)/shard_map/ppermute | solution.py:121
  21.8 2.4 %collective-permute-start.7 = (bf16[32,1024]{1,0:T(8,128)(2,1)S(1)}, bf16[32,1024]{1,0:T(8,128)(2,1)S(1)}, u32[]{:S(2)}, u32[]{:S(2)}) collective-permute-start(bf16[32,1024]{1,0:T(8,128)(2,1)S(1)} %copy-done.22), channel_id=1, source_target_pairs={{0,8},{1,9},{2,10},{3,11},{4,12},{5,13},{6,14},{7,15},{8,0},{9,1},... | collective-permute-start | bytes 196616 | tf_op jit(solution)/shard_map/ppermute | solution.py:121
  24.6 3.6 %collective-permute-start.9 = (bf16[32,1024]{1,0:T(8,128)(2,1)S(1)}, bf16[32,1024]{1,0:T(8,128)(2,1)S(1)}, u32[]{:S(2)}, u32[]{:S(2)}) collective-permute-start(bf16[32,1024]{1,0:T(8,128)(2,1)S(1)} %copy-done.20), channel_id=1, source_target_pairs={{0,10},{1,11},{2,8},{3,9},{4,14},{5,15},{6,12},{7,13},{8,2},{9,3},... | collective-permute-start | bytes 196616 | tf_op jit(solution)/shard_map/ppermute | solution.py:121
  28.2 10.4 %collective-permute-done.5 = bf16[32,1024]{1,0:T(8,128)(2,1)S(1)} collective-permute-done((bf16[32,1024]{1,0:T(8,128)(2,1)S(1)}, bf16[32,1024]{1,0:T(8,128)(2,1)S(1)}, u32[]{:S(2)}, u32[]{:S(2)}) %collective-permute-start.5) | collective-permute-done | bytes 65568 | tf_op jit(solution)/shard_map/ppermute | solution.py:121
  38.6 4.2 %collective-permute-start.10 = (bf16[32,1024]{1,0:T(8,128)(2,1)S(1)}, bf16[32,1024]{1,0:T(8,128)(2,1)S(1)}, u32[]{:S(2)}, u32[]{:S(2)}) collective-permute-start(bf16[32,1024]{1,0:T(8,128)(2,1)S(1)} %copy-done.19), channel_id=1, source_target_pairs={{0,11},{1,10},{2,9},{3,8},{4,15},{5,14},{6,13},{7,12},{8,3},{9,2},... | collective-permute-start | bytes 196616 | tf_op jit(solution)/shard_map/ppermute | solution.py:121
  42.8 1.6 %collective-permute-start.11 = (bf16[32,1024]{1,0:T(8,128)(2,1)S(1)}, bf16[32,1024]{1,0:T(8,128)(2,1)S(1)}, u32[]{:S(2)}, u32[]{:S(2)}) collective-permute-start(bf16[32,1024]{1,0:T(8,128)(2,1)S(1)} %copy-done.18), channel_id=1, source_target_pairs={{0,12},{1,13},{2,14},{3,15},{4,8},{5,9},{6,10},{7,11},{8,4},{9,5},... | collective-permute-start | bytes 196616 | tf_op jit(solution)/shard_map/ppermute | solution.py:121
  44.4 9.8 %collective-permute-done.7 = bf16[32,1024]{1,0:T(8,128)(2,1)S(1)} collective-permute-done((bf16[32,1024]{1,0:T(8,128)(2,1)S(1)}, bf16[32,1024]{1,0:T(8,128)(2,1)S(1)}, u32[]{:S(2)}, u32[]{:S(2)}) %collective-permute-start.7) | collective-permute-done | bytes 65568 | tf_op jit(solution)/shard_map/ppermute | solution.py:121
  54.4 3.1 %collective-permute-start.13 = (bf16[32,1024]{1,0:T(8,128)(2,1)S(1)}, bf16[32,1024]{1,0:T(8,128)(2,1)S(1)}, u32[]{:S(2)}, u32[]{:S(2)}) collective-permute-start(bf16[32,1024]{1,0:T(8,128)(2,1)S(1)} %copy-done.16), channel_id=1, source_target_pairs={{0,14},{1,15},{2,12},{3,13},{4,10},{5,11},{6,8},{7,9},{8,6},{9,7},... | collective-permute-start | bytes 196616 | tf_op jit(solution)/shard_map/ppermute | solution.py:121
  57.9 2.1 %collective-permute-start.14 = (bf16[32,1024]{1,0:T(8,128)(2,1)S(1)}, bf16[32,1024]{1,0:T(8,128)(2,1)S(1)}, u32[]{:S(2)}, u32[]{:S(2)}) collective-permute-start(bf16[32,1024]{1,0:T(8,128)(2,1)S(1)} %copy-done.15), channel_id=1, source_target_pairs={{0,15},{1,14},{2,13},{3,12},{4,11},{5,10},{6,9},{7,8},{8,7},{9,6},... | collective-permute-start | bytes 196616 | tf_op jit(solution)/shard_map/ppermute | solution.py:121
  60.0 1.6 %collective-permute-done.13 = bf16[32,1024]{1,0:T(8,128)(2,1)S(1)} collective-permute-done((bf16[32,1024]{1,0:T(8,128)(2,1)S(1)}, bf16[32,1024]{1,0:T(8,128)(2,1)S(1)}, u32[]{:S(2)}, u32[]{:S(2)}) %collective-permute-start.13) | collective-permute-done | bytes 65568 | tf_op jit(solution)/shard_map/ppermute | solution.py:121
  61.7 2.7 %collective-permute-done.14 = bf16[32,1024]{1,0:T(8,128)(2,1)S(1)} collective-permute-done((bf16[32,1024]{1,0:T(8,128)(2,1)S(1)}, bf16[32,1024]{1,0:T(8,128)(2,1)S(1)}, u32[]{:S(2)}, u32[]{:S(2)}) %collective-permute-start.14) | collective-permute-done | bytes 65568 | tf_op jit(solution)/shard_map/ppermute | solution.py:121
  64.8 1.6 %collective-permute-start.16 = (bf16[256,1024]{1,0:T(8,128)(2,1)S(1)}, bf16[256,1024]{1,0:T(8,128)(2,1)S(1)}, u32[]{:S(2)}, u32[]{:S(2)}) collective-permute-start(bf16[256,1024]{1,0:T(8,128)(2,1)S(1)} %convolution_convert_fusion.2), channel_id=1, source_target_pairs={{0,16},{16,0},{1,17},{17,1},{2,18},{18,2},{3,19},{19,3},{4,20},{20... | collective-permute-start | bytes 1572872 | tf_op jit(solution)/shard_map/ppermute | solution.py:114
  66.7 2.6 %fusion.6 = f32[256,2048]{1,0:T(8,128)} fusion(bf16[256,1024]{1,0:T(8,128)(2,1)S(1)} %convolution_convert_fusion.2, bf16[1,1024,2048]{2,1,0:T(8,128)(2,1)S(1)} %copy-done.13), kind=kOutput, calls=%fused_computation.6 | convolution fusion | flops 1073741824 | bytes 6815744 | tf_op jit(solution)/shard_map/dot_general | solution.py:26
  69.3 10.4 %collective-permute-done.16 = bf16[256,1024]{1,0:T(8,128)(2,1)S(1)} collective-permute-done((bf16[256,1024]{1,0:T(8,128)(2,1)S(1)}, bf16[256,1024]{1,0:T(8,128)(2,1)S(1)}, u32[]{:S(2)}, u32[]{:S(2)}) %collective-permute-start.16) | collective-permute-done | bytes 524320 | tf_op jit(solution)/shard_map/ppermute | solution.py:114
  79.9 2.6 %fusion.2 = f32[256,2048]{1,0:T(8,128)} fusion(bf16[256,1024]{1,0:T(8,128)(2,1)S(1)} %collective-permute-done.16, bf16[1,1024,2048]{2,1,0:T(8,128)(2,1)S(1)} %copy-done.13), kind=kOutput, calls=%fused_computation.2 | convolution fusion | flops 1073741824 | bytes 6815744 | tf_op jit(solution)/shard_map/dot_general | solution.py:26
  83.8 1.5 collective-permute-start.15
  85.3 5.8 %multiply_reduce_fusion.1 = (f32[256]{0:T(256)S(1)}, bf16[256,2048]{1,0:T(8,128)(2,1)}, bf16[256,2048]{1,0:T(8,128)(2,1)S(1)}) fusion(f32[256,2048]{1,0:T(8,128)S(1)} %copy-done.26, f32[256]{0:T(256)S(1)} %fusion.59, bf16[256,1024]{1,0:T(8,128)(2,1)S(1)} %get-tuple-element.65, bf16[1,2048,1024]{2,1,0:T(8,128)(2,1)} %param.11), kind=kOutput, calls=%fused_computation.40 | convolution fusion | flops 1086848768 | bytes 8914944 | tf_op jit(solution)/shard_map/dot_general | solution.py:26
  92.6 5.1 %collective-permute-done.15 = bf16[256,1024]{1,0:T(8,128)(2,1)S(1)} collective-permute-done((bf16[256,1024]{1,0:T(8,128)(2,1)S(1)}, bf16[256,1024]{1,0:T(8,128)(2,1)S(1)}, u32[]{:S(2)}, u32[]{:S(2)}) %collective-permute-start.15) | collective-permute-done | bytes 524320 | tf_op jit(solution)/shard_map/ppermute | solution.py:114
  97.7 3.8 %multiply_reduce_fusion = (f32[256]{0:T(256)S(1)}, bf16[256,2048]{1,0:T(8,128)(2,1)}, bf16[256,2048]{1,0:T(8,128)(2,1)S(1)}) fusion(f32[256,2048]{1,0:T(8,128)S(1)} %copy-done.25, f32[256]{0:T(256)S(1)} %fusion.58, bf16[256,1024]{1,0:T(8,128)(2,1)S(1)} %collective-permute-done.15, bf16[1,2048,1024]{2,1,0:T(8,128)(2,1)S(1)} %copy-done.12), kind=kOutput, calls=%fused_computation.38 | convolution fusion | flops 1086848768 | bytes 8914944 | tf_op jit(solution)/shard_map/dot_general | solution.py:26
  102.8 1.6 %collective-permute-start.17 = (bf16[256,1024]{1,0:T(8,128)(2,1)S(1)}, bf16[256,1024]{1,0:T(8,128)(2,1)}, u32[]{:S(2)}, u32[]{:S(2)}) collective-permute-start(bf16[256,1024]{1,0:T(8,128)(2,1)S(1)} %fusion.38), channel_id=1, source_target_pairs={{0,16},{16,0},{1,17},{17,1},{2,18},{18,2},{3,19},{19,3},{4,20},{20... | collective-permute-start | bytes 1572872 | tf_op jit(solution)/shard_map/ppermute | solution.py:114
  105.3 3.5 %all-to-all-start.2 = ((f32[32,1,1024]{2,1,0:T(1,128)}), f32[32,1,1024]{2,1,0:T(1,128)S(1)}, u32[]{:S(2)}, u32[]{:S(2)}) async-start(f32[32,1,1024]{2,1,0:T(1,128)} %broadcast_in_dim.15), calls=%async_computation.2 | async-start | bytes 262144 | tf_op jit(solution)/shard_map/all_to_all | solution.py:195
  108.8 8.4 %collective-permute-done.17 = bf16[256,1024]{1,0:T(8,128)(2,1)} collective-permute-done((bf16[256,1024]{1,0:T(8,128)(2,1)S(1)}, bf16[256,1024]{1,0:T(8,128)(2,1)}, u32[]{:S(2)}, u32[]{:S(2)}) %collective-permute-start.17) | collective-permute-done | bytes 524320 | tf_op jit(solution)/shard_map/ppermute | solution.py:114
  117.2 2.5 %convolution_convert_fusion = bf16[512,1024]{1,0:T(8,128)(2,1)} fusion(bf16[512,256]{1,0:T(8,128)(2,1)S(1)} %copy-done.8, f32[256,1024]{1,0:T(8,128)S(1)} %fusion.32, bf16[256,1024]{1,0:T(8,128)(2,1)} %collective-permute-done.17), kind=kOutput, calls=%fused_computation.42 | convolution fusion | flops 269746176 | bytes 2883584 | tf_op jit(solution)/shard_map/dot_general | solution.py:26
  119.8 4.2 %all-to-all-start.1 = ((bf16[16,32,1024]{2,1,0:T(8,128)(2,1)}), bf16[16,32,1024]{2,1,0:T(8,128)(2,1)S(1)}, u32[]{:S(2)}, u32[]{:S(2)}) async-start(bf16[16,32,1024]{2,1,0:T(8,128)(2,1)} %bitcast.8), calls=%async_computation.1 | async-start | bytes 2097152 | tf_op jit(solution)/shard_map/all_to_all | solution.py:127
  125.4 5.8 %convert_bitcast_fusion = bf16[1,2048,1024]{2,1,0:T(8,128)(2,1)} fusion(bf16[256,2048]{1,0:T(8,128)(2,1)} %get-tuple-element.58, bf16[256,2048]{1,0:T(8,128)(2,1)S(1)} %copy-done.31, bf16[256,1024]{1,0:T(8,128)(2,1)S(1)} %multiply_convert_fusion.2, bf16[256,1024]{1,0:T(8,128)(2,1)S(1)} %copy-done.4), kind=kOutput, calls=%fused_computation.12 | convolution fusion | flops 2155872256 | bytes 7340032 | tf_op jit(solution)/shard_map/dot_general | solution.py:26
  131.2 4.4 %convert_bitcast_fusion.1 = bf16[1,1024,2048]{2,1,0:T(8,128)(2,1)} fusion(bf16[256,2048]{1,0:T(8,128)(2,1)S(1)} %copy-done.30, bf16[256,2048]{1,0:T(8,128)(2,1)S(1)} %copy-done.28, bf16[256,1024]{1,0:T(8,128)(2,1)S(1)} %copy-done.3, bf16[256,1024]{1,0:T(8,128)(2,1)S(1)} %convolution_convert_fusion.2), kind=kOutput, calls=%fused_computation.13 | convolution fusion | flops 2155872256 | bytes 7340032 | tf_op jit(solution)/shard_map/dot_general | solution.py:26
  136.3 10.6 %all-to-all-done.1 = bf16[16,32,1024]{2,1,0:T(8,128)(2,1)S(1)} async-done(((bf16[16,32,1024]{2,1,0:T(8,128)(2,1)}), bf16[16,32,1024]{2,1,0:T(8,128)(2,1)S(1)}, u32[]{:S(2)}, u32[]{:S(2)}) %all-to-all-start.1) | async-done | bytes 1048608 | tf_op jit(solution)/shard_map/all_to_all | solution.py:127
  (125 shorter events, 12.4 us)
Async XLA Ops:
  0.6 18.1 %copy-start.11 = (bf16[1024,16]{0,1:T(8,128)(2,1)S(1)}, bf16[1024,16]{0,1:T(8,128)(2,1)}, u32[]{:S(2)}) copy-start(bf16[1024,16]{0,1:T(8,128)(2,1)} %param.9) | copy-start | bytes 98308
  4.3 19.9 %copy-start.21 = (bf16[32,1024]{1,0:T(8,128)(2,1)S(1)}, bf16[32,1024]{1,0:T(8,128)(2,1)}, u32[]{:S(2)}) copy-start(bf16[32,1024]{1,0:T(8,128)(2,1)} %get-tuple-element.41) | copy-start | bytes 196612
  4.4 20.2 %copy-start.20 = (bf16[32,1024]{1,0:T(8,128)(2,1)S(1)}, bf16[32,1024]{1,0:T(8,128)(2,1)}, u32[]{:S(2)}) copy-start(bf16[32,1024]{1,0:T(8,128)(2,1)} %get-tuple-element.42) | copy-start | bytes 196612
  4.4 34.2 %copy-start.19 = (bf16[32,1024]{1,0:T(8,128)(2,1)S(1)}, bf16[32,1024]{1,0:T(8,128)(2,1)}, u32[]{:S(2)}) copy-start(bf16[32,1024]{1,0:T(8,128)(2,1)} %get-tuple-element.43) | copy-start | bytes 196612
  4.4 38.4 %copy-start.18 = (bf16[32,1024]{1,0:T(8,128)(2,1)S(1)}, bf16[32,1024]{1,0:T(8,128)(2,1)}, u32[]{:S(2)}) copy-start(bf16[32,1024]{1,0:T(8,128)(2,1)} %get-tuple-element.44) | copy-start | bytes 196612
  4.4 49.8 %copy-start.17 = (bf16[32,1024]{1,0:T(8,128)(2,1)S(1)}, bf16[32,1024]{1,0:T(8,128)(2,1)}, u32[]{:S(2)}) copy-start(bf16[32,1024]{1,0:T(8,128)(2,1)} %get-tuple-element.45) | copy-start | bytes 196612
  4.4 50.0 %copy-start.16 = (bf16[32,1024]{1,0:T(8,128)(2,1)S(1)}, bf16[32,1024]{1,0:T(8,128)(2,1)}, u32[]{:S(2)}) copy-start(bf16[32,1024]{1,0:T(8,128)(2,1)} %get-tuple-element.46) | copy-start | bytes 196612
  4.4 14.3 %collective-permute-start = (bf16[32,1024]{1,0:T(8,128)(2,1)}, bf16[32,1024]{1,0:T(8,128)(2,1)S(1)}, u32[]{:S(2)}, u32[]{:S(2)}) collective-permute-start(bf16[32,1024]{1,0:T(8,128)(2,1)} %get-tuple-element.33), channel_id=1, source_target_pairs={{0,1},{1,0},{2,3},{3,2},{4,5},{5,4},{6,7},{7,6},{8,9},{9,8},{10,11... | collective-permute-start | bytes 196616 | tf_op jit(solution)/shard_map/ppermute | solution.py:121
  5.0 16.7 %collective-permute-start.1 = (bf16[32,1024]{1,0:T(8,128)(2,1)}, bf16[32,1024]{1,0:T(8,128)(2,1)S(1)}, u32[]{:S(2)}, u32[]{:S(2)}) collective-permute-start(bf16[32,1024]{1,0:T(8,128)(2,1)} %get-tuple-element.34), channel_id=1, source_target_pairs={{0,2},{1,3},{2,0},{3,1},{4,6},{5,7},{6,4},{7,5},{8,10},{9,11},{10,... | collective-permute-start | bytes 196616 | tf_op jit(solution)/shard_map/ppermute | solution.py:121
  7.5 14.2 %collective-permute-start.2 = (bf16[32,1024]{1,0:T(8,128)(2,1)}, bf16[32,1024]{1,0:T(8,128)(2,1)S(1)}, u32[]{:S(2)}, u32[]{:S(2)}) collective-permute-start(bf16[32,1024]{1,0:T(8,128)(2,1)} %get-tuple-element.35), channel_id=1, source_target_pairs={{0,3},{1,2},{2,1},{3,0},{4,7},{5,6},{6,5},{7,4},{8,11},{9,10},{10,... | collective-permute-start | bytes 196616 | tf_op jit(solution)/shard_map/ppermute | solution.py:121
  7.6 16.6 %collective-permute-start.3 = (bf16[32,1024]{1,0:T(8,128)(2,1)}, bf16[32,1024]{1,0:T(8,128)(2,1)S(1)}, u32[]{:S(2)}, u32[]{:S(2)}) collective-permute-start(bf16[32,1024]{1,0:T(8,128)(2,1)} %get-tuple-element.36), channel_id=1, source_target_pairs={{0,4},{1,5},{2,6},{3,7},{4,0},{5,1},{6,2},{7,3},{8,12},{9,13},{10,... | collective-permute-start | bytes 196616 | tf_op jit(solution)/shard_map/ppermute | solution.py:121
  9.4 15.2 %collective-permute-start.4 = (bf16[32,1024]{1,0:T(8,128)(2,1)}, bf16[32,1024]{1,0:T(8,128)(2,1)S(1)}, u32[]{:S(2)}, u32[]{:S(2)}) collective-permute-start(bf16[32,1024]{1,0:T(8,128)(2,1)} %get-tuple-element.37), channel_id=1, source_target_pairs={{0,5},{1,4},{2,7},{3,6},{4,1},{5,0},{6,3},{7,2},{8,13},{9,12},{10,... | collective-permute-start | bytes 196616 | tf_op jit(solution)/shard_map/ppermute | solution.py:121
  9.4 48.5 %copy-start.15 = (bf16[32,1024]{1,0:T(8,128)(2,1)S(1)}, bf16[32,1024]{1,0:T(8,128)(2,1)}, u32[]{:S(2)}) copy-start(bf16[32,1024]{1,0:T(8,128)(2,1)} %get-tuple-element.47) | copy-start | bytes 196612
  12.4 52.0 %copy-start.6 = (bf16[256,512]{1,0:T(8,128)(2,1)S(1)}, bf16[256,512]{1,0:T(8,128)(2,1)}, u32[]{:S(2)}) copy-start(bf16[256,512]{1,0:T(8,128)(2,1)} %get-tuple-element.31) | copy-start | bytes 786436
  12.4 70.1 %all-to-all-start = ((bf16[16,32,1024]{2,1,0:T(8,128)(2,1)}), bf16[16,32,1024]{2,1,0:T(8,128)(2,1)S(1)}, u32[]{:S(2)}, u32[]{:S(2)}) async-start(bf16[16,32,1024]{2,1,0:T(8,128)(2,1)} %bitcast.61), calls=%async_computation | async-start | bytes 2097152 | tf_op jit(solution)/shard_map/all_to_all | solution.py:127
  18.7 19.8 %collective-permute-start.5 = (bf16[32,1024]{1,0:T(8,128)(2,1)S(1)}, bf16[32,1024]{1,0:T(8,128)(2,1)S(1)}, u32[]{:S(2)}, u32[]{:S(2)}) collective-permute-start(bf16[32,1024]{1,0:T(8,128)(2,1)S(1)} %copy-done.24), channel_id=1, source_target_pairs={{0,6},{1,7},{2,4},{3,5},{4,2},{5,3},{6,0},{7,1},{8,14},{9,15},{10,... | collective-permute-start | bytes 196616 | tf_op jit(solution)/shard_map/ppermute | solution.py:121
  21.6 45.0 %copy-start.13 = (bf16[1,1024,2048]{2,1,0:T(8,128)(2,1)S(1)}, bf16[1,1024,2048]{2,1,0:T(8,128)(2,1)}, u32[]{:S(2)}) copy-start(bf16[1,1024,2048]{2,1,0:T(8,128)(2,1)} %param.10) | copy-start | bytes 12582916
  21.7 21.1 %collective-permute-start.6 = (bf16[32,1024]{1,0:T(8,128)(2,1)S(1)}, bf16[32,1024]{1,0:T(8,128)(2,1)S(1)}, u32[]{:S(2)}, u32[]{:S(2)}) collective-permute-start(bf16[32,1024]{1,0:T(8,128)(2,1)S(1)} %copy-done.23), channel_id=1, source_target_pairs={{0,7},{1,6},{2,5},{3,4},{4,3},{5,2},{6,1},{7,0},{8,15},{9,14},{10,... | collective-permute-start | bytes 196616 | tf_op jit(solution)/shard_map/ppermute | solution.py:121
  21.8 32.4 %collective-permute-start.7 = (bf16[32,1024]{1,0:T(8,128)(2,1)S(1)}, bf16[32,1024]{1,0:T(8,128)(2,1)S(1)}, u32[]{:S(2)}, u32[]{:S(2)}) collective-permute-start(bf16[32,1024]{1,0:T(8,128)(2,1)S(1)} %copy-done.22), channel_id=1, source_target_pairs={{0,8},{1,9},{2,10},{3,11},{4,12},{5,13},{6,14},{7,15},{8,0},{9,1},... | collective-permute-start | bytes 196616 | tf_op jit(solution)/shard_map/ppermute | solution.py:121
  24.2 30.2 %collective-permute-start.8 = (bf16[32,1024]{1,0:T(8,128)(2,1)S(1)}, bf16[32,1024]{1,0:T(8,128)(2,1)S(1)}, u32[]{:S(2)}, u32[]{:S(2)}) collective-permute-start(bf16[32,1024]{1,0:T(8,128)(2,1)S(1)} %copy-done.21), channel_id=1, source_target_pairs={{0,9},{1,8},{2,11},{3,10},{4,13},{5,12},{6,15},{7,14},{8,1},{9,0},... | collective-permute-start | bytes 196616 | tf_op jit(solution)/shard_map/ppermute | solution.py:121
  24.6 33.3 %collective-permute-start.9 = (bf16[32,1024]{1,0:T(8,128)(2,1)S(1)}, bf16[32,1024]{1,0:T(8,128)(2,1)S(1)}, u32[]{:S(2)}, u32[]{:S(2)}) collective-permute-start(bf16[32,1024]{1,0:T(8,128)(2,1)S(1)} %copy-done.20), channel_id=1, source_target_pairs={{0,10},{1,11},{2,8},{3,9},{4,14},{5,15},{6,12},{7,13},{8,2},{9,3},... | collective-permute-start | bytes 196616 | tf_op jit(solution)/shard_map/ppermute | solution.py:121
  38.6 21.4 %collective-permute-start.10 = (bf16[32,1024]{1,0:T(8,128)(2,1)S(1)}, bf16[32,1024]{1,0:T(8,128)(2,1)S(1)}, u32[]{:S(2)}, u32[]{:S(2)}) collective-permute-start(bf16[32,1024]{1,0:T(8,128)(2,1)S(1)} %copy-done.19), channel_id=1, source_target_pairs={{0,11},{1,10},{2,9},{3,8},{4,15},{5,14},{6,13},{7,12},{8,3},{9,2},... | collective-permute-start | bytes 196616 | tf_op jit(solution)/shard_map/ppermute | solution.py:121
  42.8 17.2 %collective-permute-start.11 = (bf16[32,1024]{1,0:T(8,128)(2,1)S(1)}, bf16[32,1024]{1,0:T(8,128)(2,1)S(1)}, u32[]{:S(2)}, u32[]{:S(2)}) collective-permute-start(bf16[32,1024]{1,0:T(8,128)(2,1)S(1)} %copy-done.18), channel_id=1, source_target_pairs={{0,12},{1,13},{2,14},{3,15},{4,8},{5,9},{6,10},{7,11},{8,4},{9,5},... | collective-permute-start | bytes 196616 | tf_op jit(solution)/shard_map/ppermute | solution.py:121
  54.2 5.8 %collective-permute-start.12 = (bf16[32,1024]{1,0:T(8,128)(2,1)S(1)}, bf16[32,1024]{1,0:T(8,128)(2,1)S(1)}, u32[]{:S(2)}, u32[]{:S(2)}) collective-permute-start(bf16[32,1024]{1,0:T(8,128)(2,1)S(1)} %copy-done.17), channel_id=1, source_target_pairs={{0,13},{1,12},{2,15},{3,14},{4,9},{5,8},{6,11},{7,10},{8,5},{9,4},... | collective-permute-start | bytes 196616 | tf_op jit(solution)/shard_map/ppermute | solution.py:121
  54.4 7.2 %collective-permute-start.13 = (bf16[32,1024]{1,0:T(8,128)(2,1)S(1)}, bf16[32,1024]{1,0:T(8,128)(2,1)S(1)}, u32[]{:S(2)}, u32[]{:S(2)}) collective-permute-start(bf16[32,1024]{1,0:T(8,128)(2,1)S(1)} %copy-done.16), channel_id=1, source_target_pairs={{0,14},{1,15},{2,12},{3,13},{4,10},{5,11},{6,8},{7,9},{8,6},{9,7},... | collective-permute-start | bytes 196616 | tf_op jit(solution)/shard_map/ppermute | solution.py:121
  57.9 6.5 %collective-permute-start.14 = (bf16[32,1024]{1,0:T(8,128)(2,1)S(1)}, bf16[32,1024]{1,0:T(8,128)(2,1)S(1)}, u32[]{:S(2)}, u32[]{:S(2)}) collective-permute-start(bf16[32,1024]{1,0:T(8,128)(2,1)S(1)} %copy-done.15), channel_id=1, source_target_pairs={{0,15},{1,14},{2,13},{3,12},{4,11},{5,10},{6,9},{7,8},{8,7},{9,6},... | collective-permute-start | bytes 196616 | tf_op jit(solution)/shard_map/ppermute | solution.py:121
  64.8 14.8 %collective-permute-start.16 = (bf16[256,1024]{1,0:T(8,128)(2,1)S(1)}, bf16[256,1024]{1,0:T(8,128)(2,1)S(1)}, u32[]{:S(2)}, u32[]{:S(2)}) collective-permute-start(bf16[256,1024]{1,0:T(8,128)(2,1)S(1)} %convolution_convert_fusion.2), channel_id=1, source_target_pairs={{0,16},{16,0},{1,17},{17,1},{2,18},{18,2},{3,19},{19,3},{4,20},{20... | collective-permute-start | bytes 1572872 | tf_op jit(solution)/shard_map/ppermute | solution.py:114
  79.6 24.7 %copy-start.2 = (bf16[256,1024]{1,0:T(8,128)(2,1)}, bf16[256,1024]{1,0:T(8,128)(2,1)S(1)}, u32[]{:S(2)}) copy-start(bf16[256,1024]{1,0:T(8,128)(2,1)S(1)} %collective-permute-done.16) | copy-start | bytes 1572868
  83.8 13.9 %collective-permute-start.15 = (bf16[256,1024]{1,0:T(8,128)(2,1)S(1)}, bf16[256,1024]{1,0:T(8,128)(2,1)S(1)}, u32[]{:S(2)}, u32[]{:S(2)}) collective-permute-start(bf16[256,1024]{1,0:T(8,128)(2,1)S(1)} %get-tuple-element.65), channel_id=1, source_target_pairs={{0,16},{16,0},{1,17},{17,1},{2,18},{18,2},{3,19},{19,3},{4,20},{20... | collective-permute-start | bytes 1572872 | tf_op jit(solution)/shard_map/ppermute | solution.py:114
  102.8 14.4 %collective-permute-start.17 = (bf16[256,1024]{1,0:T(8,128)(2,1)S(1)}, bf16[256,1024]{1,0:T(8,128)(2,1)}, u32[]{:S(2)}, u32[]{:S(2)}) collective-permute-start(bf16[256,1024]{1,0:T(8,128)(2,1)S(1)} %fusion.38), channel_id=1, source_target_pairs={{0,16},{16,0},{1,17},{17,1},{2,18},{18,2},{3,19},{19,3},{4,20},{20... | collective-permute-start | bytes 1572872 | tf_op jit(solution)/shard_map/ppermute | solution.py:114
  105.3 14.5 %all-to-all-start.2 = ((f32[32,1,1024]{2,1,0:T(1,128)}), f32[32,1,1024]{2,1,0:T(1,128)S(1)}, u32[]{:S(2)}, u32[]{:S(2)}) async-start(f32[32,1,1024]{2,1,0:T(1,128)} %broadcast_in_dim.15), calls=%async_computation.2 | async-start | bytes 262144 | tf_op jit(solution)/shard_map/all_to_all | solution.py:195
  119.8 27.1 %all-to-all-start.1 = ((bf16[16,32,1024]{2,1,0:T(8,128)(2,1)}), bf16[16,32,1024]{2,1,0:T(8,128)(2,1)S(1)}, u32[]{:S(2)}, u32[]{:S(2)}) async-start(bf16[16,32,1024]{2,1,0:T(8,128)(2,1)} %bitcast.8), calls=%async_computation.1 | async-start | bytes 2097152 | tf_op jit(solution)/shard_map/all_to_all | solution.py:127
  (21 other events, 166.6 us)
where the time goes:
time: 151 us; the launch traced here: 150 us
  waiting for transfers between devices  59.5 us (39%)
  starting transfers between devices  43.8 us (29%)
  matrix products  33.2 us (22%)
  Pallas kernels  6.69 us (4%)
  other arithmetic  3.52 us (2%)
  local copies, waits for them, and re-layouts  1.71 us (1%)
    dot_general x14, matrix products, contract(): lax.dot_general(left, right, (((left_dim,), (right_dim,)), ((), ())), pre...  33.2 us
    ppermute x15, starting transfers between devices, pairwise(): lax.ppermute(blocks[k], 'expert', [(i, i ^ k) for i in range(count)])  25.3 us
    ppermute x15, waiting for transfers between devices, pairwise(): lax.ppermute(blocks[k], 'expert', [(i, i ^ k) for i in range(count)])  25.1 us
    ppermute x3, waiting for transfers between devices, swap_dp(): lax.ppermute(values, 'dp', [(i, count - 1 - i) for i in range(count)])  23.9 us
    all_to_all x2, waiting for transfers between devices, exchange(): lax.all_to_all(blocks, 'expert', 0, 0, tiled=True).reshape(rows.shape)  10.6 us
    all_to_all x2, starting transfers between devices, exchange(): lax.all_to_all(blocks, 'expert', 0, 0, tiled=True).reshape(rows.shape)  10.4 us
    ppermute x3, starting transfers between devices, swap_dp(): lax.ppermute(values, 'dp', [(i, count - 1 - i) for i in range(count)])  4.61 us
    pallas_call x1, Pallas kernels, body(): pl.pallas_call(prep_u_kernel, in_specs=[scalar_spec] + [pl.BlockSpec()] *...  3.67 us
  transfers between devices with their start and end apart: 21, of which 10 were waited for; matrix products, arithmetic and copies ran while one was open for 19% of the time, Pallas kernels for 2%

commit v1 on v0

--- a/solution.py
+++ b/solution.py
@@ -74,14 +74,14 @@
         [one_hot(slot_ref[pl.ds(me ^ k, 1), :]) for k in range(experts)], axis=0
     )
     sent = contract(crossed, normal_u, 1, 0).astype(bf16)
-    for k in range(experts):
-        u_outs[k][...] = sent[k * most : (k + 1) * most]
+    for k in range(len(u_outs)):
+        u_outs[k][...] = sent[2 * k * most : 2 * (k + 1) * most]
     for e in range(experts):
         select_ref[e * most : (e + 1) * most, :] = one_hot(slot[e : e + 1])
 
 
 def prep_g_kernel(most, me_ref, chosen_ref, select_ref, grad_ref, g_out, u_place, g_place, spread):
-    _, cap = chosen_ref.shape
+    experts, cap = chosen_ref.shape
     slots, tok_count = select_ref.shape
     me = me_ref[0]
     g_out[...] = contract(select_ref[...], grad_ref[...], 1, 0).astype(bf16)
@@ -99,7 +99,9 @@
         place = jnp.where(offset < count, start + offset, -1)
         return (iota((cap, slots), 0) == place).astype(f32)
 
-    u_place[...] = places(block ^ me).astype(bf16)
+    half = experts // 2
+    turn = jnp.where(block < half, 2 * block, 2 * (block - half) + 1)
+    u_place[...] = places(turn ^ me).astype(bf16)
     ordered = places(block)
     g_place[...] = ordered.astype(bf16)
     spread[...] = jnp.transpose(ordered).astype(bf16)
@@ -114,12 +116,16 @@
     return lax.ppermute(values, "dp", [(i, count - 1 - i) for i in range(count)])
 
 
-def pairwise(blocks):
-    count = len(blocks)
-    got = {0: blocks[0]}
-    for k in range(count - 1, 0, -1):
-        got[k] = lax.ppermute(blocks[k], "expert", [(i, i ^ k) for i in range(count)])
-    return jnp.concatenate([got[k] for k in range(count)], axis=0)
+def pairwise(pairs):
+    count = lax.axis_size("expert")
+    most = pairs[0].shape[0] // 2
+    got = {0: pairs[0]}
+    for k in range(len(pairs) - 1, 0, -1):
+        got[k] = lax.ppermute(pairs[k], "expert", [(i, i ^ (2 * k)) for i in range(count)])
+    got = [got[k] for k in range(len(pairs))]
+    passed = jnp.concatenate([pair[most:] for pair in got], axis=0)
+    passed = lax.ppermute(passed, "expert", [(i, i ^ 1) for i in range(count)])
+    return jnp.concatenate([pair[:most] for pair in got] + [passed], axis=0)
 
 
 def exchange(rows, experts):
@@ -146,7 +152,6 @@
 def body(tokens, modulation, router_weight, weight_in, weight_out, chosen, grad_out):
     tok_count, width = tokens.shape
     experts = lax.axis_size("expert")
-    halves = lax.axis_size("dp")
     most = 2 * tok_count // experts
     cap = chosen.shape[2]
     me = lax.axis_index("expert").astype(i32)
@@ -156,7 +161,8 @@
     *u_blocks, select = pl.pallas_call(
         prep_u_kernel,
         in_specs=[scalar_spec] + [pl.BlockSpec()] * 3,
-        out_shape=[shape((most, width), bf16)] * experts + [shape((slots, tok_count), bf16)],
+        out_shape=[shape((2 * most, width), bf16)] * (experts // 2)
+        + [shape((slots, tok_count), bf16)],
         scratch_shapes=[pltpu.VMEM((experts, tok_count), i32)],
         compiler_params=big,
         name="prep_u",
@@ -190,13 +196,13 @@
     )
 
     total = (back_own + swap_dp(back_other.astype(bf16)).astype(f32)).astype(bf16)
+    total = lax.optimization_barrier(total)
     returned = exchange(contract(spread, total, 1, 0).astype(bf16), experts)
 
     columns = lax.all_to_all(
-        jnp.broadcast_to(column_own + column_other, (halves * experts, width)),
-        ("dp", "expert"), 0, 0, tiled=True,
-    )
-    grad_router = jnp.sum(columns.reshape(halves, experts, width), axis=0).T
+        jnp.broadcast_to(column_own + column_other, (experts, width)), "expert", 0, 0, tiled=True
+    )
+    grad_router = (columns + swap_dp(columns)).T
 
     rows_u = jnp.concatenate([u_own, u_other], axis=0)
     hidden = jnp.concatenate([hidden_own, hidden_other], axis=0)

time: 151 us -> 136 us (0.901)
  waiting for transfers between devices: 59.5 us -> 45.7 us
  starting transfers between devices: 43.8 us -> 39.9 us
  matrix products: 33.2 us -> 35.1 us
    ppermute x15 -> x8, waiting for transfers between devices: 25.1 us -> 13 us  [the longest x7 13 us: pairwise(): lax.ppermute(pairs[k], 'expert', [(i, i ^ 2 * k) for i in range(count)])]
    ppermute x15 -> x8, starting transfers between devices: 25.3 us -> 13.3 us  [the longest x7 13.2 us: pairwise(): lax.ppermute(pairs[k], 'expert', [(i, i ^ 2 * k) for i in range(count)])]
    ppermute x3 -> x4, waiting for transfers between devices: 23.9 us -> 18.3 us  [swap_dp(): lax.ppermute(values, 'dp', [(i, count - 1 - i) for i in range(count)])]
    all_to_all x2, starting transfers between devices: 10.4 us -> 14.1 us  [exchange(): lax.all_to_all(blocks, 'expert', 0, 0, tiled=True).reshape(rows.shape)]
    all_to_all x2, waiting for transfers between devices: 10.6 us -> 14.2 us  [exchange(): lax.all_to_all(blocks, 'expert', 0, 0, tiled=True).reshape(rows.shape)]
    all_to_all x1, starting transfers between devices: 3.49 us -> 6.48 us  [body(): lax.all_to_all(jnp.broadcast_to(column_own + column_other, (experts, widt...]
    dot_general x14, matrix products: 33.2 us -> 35.1 us  [contract(): lax.dot_general(left, right, (((left_dim,), (right_dim,)), ((), ())), pre...]
    ppermute x3 -> x4, starting transfers between devices: 4.61 us -> 6.09 us  [swap_dp(): lax.ppermute(values, 'dp', [(i, count - 1 - i) for i in range(count)])]
  transfers between devices with their start and end apart: 21 -> 15, of which waited for: 10 -> 8; matrix products, arithmetic and copies ran while one was open for 19% -> 23% of each run, Pallas kernels for 2% -> 2%
where the time goes in v1:
time: 136 us; the launch traced here: 135 us
  waiting for transfers between devices  45.7 us (34%)
  starting transfers between devices  39.9 us (29%)
  matrix products  35.1 us (26%)
  Pallas kernels  6.67 us (5%)
  other arithmetic  3.67 us (3%)
  local copies, waits for them, and re-layouts  2.49 us (2%)
    dot_general x14, matrix products, contract(): lax.dot_general(left, right, (((left_dim,), (right_dim,)), ((), ())), pre...  35.1 us
    ppermute x4, waiting for transfers between devices, swap_dp(): lax.ppermute(values, 'dp', [(i, count - 1 - i) for i in range(count)])  18.3 us
    all_to_all x2, waiting for transfers between devices, exchange(): lax.all_to_all(blocks, 'expert', 0, 0, tiled=True).reshape(rows.shape)  14.2 us
    all_to_all x2, starting transfers between devices, exchange(): lax.all_to_all(blocks, 'expert', 0, 0, tiled=True).reshape(rows.shape)  14.1 us
    ppermute x7, starting transfers between devices, pairwise(): lax.ppermute(pairs[k], 'expert', [(i, i ^ 2 * k) for i in range(count)])  13.2 us
    ppermute x7, waiting for transfers between devices, pairwise(): lax.ppermute(pairs[k], 'expert', [(i, i ^ 2 * k) for i in range(count)])  13 us
    all_to_all x1, starting transfers between devices, body(): lax.all_to_all(jnp.broadcast_to(column_own + column_other, (experts, widt...  6.48 us
    ppermute x4, starting transfers between devices, swap_dp(): lax.ppermute(values, 'dp', [(i, count - 1 - i) for i in range(count)])  6.09 us
  transfers between devices with their start and end apart: 15, of which 8 were waited for; matrix products, arithmetic and copies ran while one was open for 23% of the time, Pallas kernels for 2%

profile of v1, /device:TPU:0, one launch (start us, length us, event | category | flops | bytes accessed | tf_op | source)
XLA Modules:
  0.0 134.6 jit_solution(13940740411294245209)
XLA Ops:
  0.6 3.7 %prep_u.1 = (bf16[64,1024]{1,0:T(8,128)(2,1)}, bf16[64,1024]{1,0:T(8,128)(2,1)}, bf16[64,1024]{1,0:T(8,128)(2,1)}, bf16[64,1024]{1,0:T(8,128)(2,1)}, bf16[64,102...) custom-call(s32[1]{0:T(128)} %bitcast.me_ref, ...), custom_call_target="tpu_custom_call" | custom-call | tf_op jit(solution)/shard_map/prep_u/pallas_call | solution.py:161
  4.3 3.0 %collective-permute-start = (bf16[64,1024]{1,0:T(8,128)(2,1)}, bf16[64,1024]{1,0:T(8,128)(2,1)S(1)}, u32[]{:S(2)}, u32[]{:S(2)}) collective-permute-start(bf16[64,1024]{1,0:T(8,128)(2,1)} %get-tuple-element.25), channel_id=1, source_target_pairs={{0,2},{1,3},{2,0},{3,1},{4,6},{5,7},{6,4},{7,5},{8,10},{9,11},{10,... | collective-permute-start | bytes 393224 | tf_op jit(solution)/shard_map/ppermute | solution.py:124
  7.3 1.6 %collective-permute-start.1 = (bf16[64,1024]{1,0:T(8,128)(2,1)}, bf16[64,1024]{1,0:T(8,128)(2,1)S(1)}, u32[]{:S(2)}, u32[]{:S(2)}) collective-permute-start(bf16[64,1024]{1,0:T(8,128)(2,1)} %get-tuple-element.26), channel_id=1, source_target_pairs={{0,4},{1,5},{2,6},{3,7},{4,0},{5,1},{6,2},{7,3},{8,12},{9,13},{10,... | collective-permute-start | bytes 393224 | tf_op jit(solution)/shard_map/ppermute | solution.py:124
  8.9 3.0 %collective-permute-start.3 = (bf16[64,1024]{1,0:T(8,128)(2,1)}, bf16[64,1024]{1,0:T(8,128)(2,1)S(1)}, u32[]{:S(2)}, u32[]{:S(2)}) collective-permute-start(bf16[64,1024]{1,0:T(8,128)(2,1)} %get-tuple-element.28), channel_id=1, source_target_pairs={{0,8},{1,9},{2,10},{3,11},{4,12},{5,13},{6,14},{7,15},{8,0},{9,1},... | collective-permute-start | bytes 393224 | tf_op jit(solution)/shard_map/ppermute | solution.py:124
  11.8 1.3 collective-permute-start.4
  13.1 0.9 slice_dynamic-update-slice_fusion.14
  14.0 3.7 %collective-permute-start.5 = (bf16[64,1024]{1,0:T(8,128)(2,1)}, bf16[64,1024]{1,0:T(8,128)(2,1)S(1)}, u32[]{:S(2)}, u32[]{:S(2)}) collective-permute-start(bf16[64,1024]{1,0:T(8,128)(2,1)} %get-tuple-element.30), channel_id=1, source_target_pairs={{0,12},{1,13},{2,14},{3,15},{4,8},{5,9},{6,10},{7,11},{8,4},{9,5},... | collective-permute-start | bytes 393224 | tf_op jit(solution)/shard_map/ppermute | solution.py:124
  19.0 12.5 %collective-permute-done.4 = bf16[64,1024]{1,0:T(8,128)(2,1)S(1)} collective-permute-done((bf16[64,1024]{1,0:T(8,128)(2,1)}, bf16[64,1024]{1,0:T(8,128)(2,1)S(1)}, u32[]{:S(2)}, u32[]{:S(2)}) %collective-permute-start.4) | collective-permute-done | bytes 131104 | tf_op jit(solution)/shard_map/ppermute | solution.py:124
  31.7 3.0 %prep_g.1 = (bf16[512,1024]{1,0:T(8,128)(2,1)}, bf16[256,512]{1,0:T(8,128)(2,1)}, bf16[256,512]{1,0:T(8,128)(2,1)}, bf16[512,256]{1,0:T(8,128)(2,1)}) custom-call(s32[1]{0:T(128)} %bitcast.me_ref, s32[16,256]{1,0:T(8,128)} %bitcast.70, bf16[512,256]{1,0:T(8,128)(2,1)} %get-tuple-element.21.select_ref, bf16[256,1024]{1,0:T(8,128)(2,1)} %grad_ref.1), custom_call_target="tpu_custom_call" | custom-call | tf_op jit(solution)/shard_map/prep_g/pallas_call | solution.py:170
  34.7 8.1 %all-to-all-start = ((bf16[16,32,1024]{2,1,0:T(8,128)(2,1)}), bf16[16,32,1024]{2,1,0:T(8,128)(2,1)S(1)}, u32[]{:S(2)}, u32[]{:S(2)}) async-start(bf16[16,32,1024]{2,1,0:T(8,128)(2,1)} %bitcast.68), calls=%async_computation | async-start | bytes 2097152 | tf_op jit(solution)/shard_map/all_to_all | solution.py:133
  43.4 1.6 %collective-permute-start.9 = (bf16[256,1024]{1,0:T(8,128)(2,1)S(1)}, bf16[256,1024]{1,0:T(8,128)(2,1)S(1)}, u32[]{:S(2)}, u32[]{:S(2)}) collective-permute-start(bf16[256,1024]{1,0:T(8,128)(2,1)S(1)} %convolution_convert_fusion.2), channel_id=1, source_target_pairs={{0,16},{16,0},{1,17},{17,1},{2,18},{18,2},{3,19},{19,3},{4,20},{20... | collective-permute-start | bytes 1572872 | tf_op jit(solution)/shard_map/ppermute | solution.py:116
  45.2 4.9 %fusion.6 = f32[256,2048]{1,0:T(8,128)} fusion(bf16[256,1024]{1,0:T(8,128)(2,1)S(1)} %convolution_convert_fusion.2, bf16[1,1024,2048]{2,1,0:T(8,128)(2,1)} %param.10), kind=kOutput, calls=%fused_computation.6 | convolution fusion | flops 1073741824 | bytes 6815744 | tf_op jit(solution)/shard_map/dot_general | solution.py:26
  50.1 7.5 %collective-permute-done.9 = bf16[256,1024]{1,0:T(8,128)(2,1)S(1)} collective-permute-done((bf16[256,1024]{1,0:T(8,128)(2,1)S(1)}, bf16[256,1024]{1,0:T(8,128)(2,1)S(1)}, u32[]{:S(2)}, u32[]{:S(2)}) %collective-permute-start.9) | collective-permute-done | bytes 524320 | tf_op jit(solution)/shard_map/ppermute | solution.py:116
  58.0 2.6 %fusion.2 = f32[256,2048]{1,0:T(8,128)} fusion(bf16[256,1024]{1,0:T(8,128)(2,1)S(1)} %collective-permute-done.9, bf16[1,1024,2048]{2,1,0:T(8,128)(2,1)S(1)} %copy-done.10), kind=kOutput, calls=%fused_computation.2 | convolution fusion | flops 1073741824 | bytes 6815744 | tf_op jit(solution)/shard_map/dot_general | solution.py:26
  60.6 5.1 %all-to-all-done = bf16[16,32,1024]{2,1,0:T(8,128)(2,1)S(1)} async-done(((bf16[16,32,1024]{2,1,0:T(8,128)(2,1)}), bf16[16,32,1024]{2,1,0:T(8,128)(2,1)S(1)}, u32[]{:S(2)}, u32[]{:S(2)}) %all-to-all-start) | async-done | bytes 1048608 | tf_op jit(solution)/shard_map/all_to_all | solution.py:133
  65.7 1.2 multiply_convert_fusion.3
  66.9 1.5 %collective-permute-start.8 = (bf16[256,1024]{1,0:T(8,128)(2,1)S(1)}, bf16[256,1024]{1,0:T(8,128)(2,1)S(1)}, u32[]{:S(2)}, u32[]{:S(2)}) collective-permute-start(bf16[256,1024]{1,0:T(8,128)(2,1)S(1)} %get-tuple-element.65), channel_id=1, source_target_pairs={{0,16},{16,0},{1,17},{17,1},{2,18},{18,2},{3,19},{19,3},{4,20},{20... | collective-permute-start | bytes 1572872 | tf_op jit(solution)/shard_map/ppermute | solution.py:116
  68.4 5.8 %multiply_reduce_fusion.1 = (f32[256]{0:T(256)S(1)}, bf16[256,2048]{1,0:T(8,128)(2,1)}, bf16[256,2048]{1,0:T(8,128)(2,1)S(1)}) fusion(f32[256,2048]{1,0:T(8,128)S(1)} %copy-done.13, f32[256]{0:T(256)S(1)} %fusion.59, bf16[256,1024]{1,0:T(8,128)(2,1)S(1)} %get-tuple-element.65, bf16[1,2048,1024]{2,1,0:T(8,128)(2,1)} %param.11), kind=kOutput, calls=%fused_computation.40 | convolution fusion | flops 1086848768 | bytes 8914944 | tf_op jit(solution)/shard_map/dot_general | solution.py:26
  74.5 1.3 fusion.32
  75.8 5.7 %collective-permute-done.8 = bf16[256,1024]{1,0:T(8,128)(2,1)S(1)} collective-permute-done((bf16[256,1024]{1,0:T(8,128)(2,1)S(1)}, bf16[256,1024]{1,0:T(8,128)(2,1)S(1)}, u32[]{:S(2)}, u32[]{:S(2)}) %collective-permute-start.8) | collective-permute-done | bytes 524320 | tf_op jit(solution)/shard_map/ppermute | solution.py:116
  81.5 3.8 %multiply_reduce_fusion = (f32[256]{0:T(256)S(1)}, bf16[256,2048]{1,0:T(8,128)(2,1)}, bf16[256,2048]{1,0:T(8,128)(2,1)S(1)}) fusion(f32[256,2048]{1,0:T(8,128)S(1)} %copy-done.12, f32[256]{0:T(256)S(1)} %fusion.58, bf16[256,1024]{1,0:T(8,128)(2,1)S(1)} %collective-permute-done.8, bf16[1,2048,1024]{2,1,0:T(8,128)(2,1)S(1)} %copy-done.9), kind=kOutput, calls=%fused_computation.38 | convolution fusion | flops 1086848768 | bytes 8914944 | tf_op jit(solution)/shard_map/dot_general | solution.py:26
  85.3 2.1 %fusion.38 = bf16[256,1024]{1,0:T(8,128)(2,1)} fusion(bf16[256,2048]{1,0:T(8,128)(2,1)S(1)} %get-tuple-element.45, bf16[1,1024,2048]{2,1,0:T(8,128)(2,1)S(1)} %copy-done.11, f32[256]{0:T(256)S(1)} %subtract_multiply_fusion, f32[1024]{0:T(1024)S(1)} %bitcast.76), kind=kOutput, calls=%fused_computation.47 | convolution fusion | flops 1074528256 | bytes 5772288 | tf_op jit(solution)/shard_map/dot_general | solution.py:26
  87.4 1.5 %collective-permute-start.10 = (bf16[256,1024]{1,0:T(8,128)(2,1)}, bf16[256,1024]{1,0:T(8,128)(2,1)S(1)}, u32[]{:S(2)}, u32[]{:S(2)}) collective-permute-start(bf16[256,1024]{1,0:T(8,128)(2,1)} %fusion.38), channel_id=1, source_target_pairs={{0,16},{16,0},{1,17},{17,1},{2,18},{18,2},{3,19},{19,3},{4,20},{20... | collective-permute-start | bytes 1572872 | tf_op jit(solution)/shard_map/ppermute | solution.py:116
  89.8 6.5 %all-to-all-start.2 = ((f32[16,1,1024]{2,1,0:T(1,128)}), f32[16,1,1024]{2,1,0:T(1,128)S(1)}, u32[]{:S(2)}, u32[]{:S(2)}) async-start(f32[16,1,1024]{2,1,0:T(1,128)} %broadcast_in_dim.15), calls=%async_computation.2 | async-start | bytes 131072 | tf_op jit(solution)/shard_map/all_to_all | solution.py:202
  96.3 5.1 %collective-permute-done.10 = bf16[256,1024]{1,0:T(8,128)(2,1)S(1)} collective-permute-done((bf16[256,1024]{1,0:T(8,128)(2,1)}, bf16[256,1024]{1,0:T(8,128)(2,1)S(1)}, u32[]{:S(2)}, u32[]{:S(2)}) %collective-permute-start.10) | collective-permute-done | bytes 524320 | tf_op jit(solution)/shard_map/ppermute | solution.py:116
  101.5 1.4 %convolution_convert_fusion = bf16[512,1024]{1,0:T(8,128)(2,1)} fusion(bf16[512,256]{1,0:T(8,128)(2,1)S(1)} %copy-done.3, bf16[256,1024]{1,0:T(8,128)(2,1)S(1)} %add_convert_fusion), kind=kOutput, calls=%fused_computation.42 | convolution fusion | flops 268959744 | bytes 1835008 | tf_op jit(solution)/shard_map/dot_general | solution.py:26
  103.2 5.9 %all-to-all-start.1 = ((bf16[16,32,1024]{2,1,0:T(8,128)(2,1)}), bf16[16,32,1024]{2,1,0:T(8,128)(2,1)S(1)}, u32[]{:S(2)}, u32[]{:S(2)}) async-start(bf16[16,32,1024]{2,1,0:T(8,128)(2,1)} %bitcast.8), calls=%async_computation.1 | async-start | bytes 2097152 | tf_op jit(solution)/shard_map/all_to_all | solution.py:133
  110.5 5.8 %convert_bitcast_fusion = bf16[1,2048,1024]{2,1,0:T(8,128)(2,1)} fusion(bf16[256,2048]{1,0:T(8,128)(2,1)} %get-tuple-element.42, bf16[256,2048]{1,0:T(8,128)(2,1)S(1)} %copy-done.18, bf16[256,1024]{1,0:T(8,128)(2,1)S(1)} %multiply_convert_fusion.2, bf16[256,1024]{1,0:T(8,128)(2,1)S(1)} %copy-done.2), kind=kOutput, calls=%fused_computation.12 | convolution fusion | flops 2155872256 | bytes 7340032 | tf_op jit(solution)/shard_map/dot_general | solution.py:26
  116.3 1.6 %collective-permute-start.11 = (f32[16,1024]{1,0:T(8,128)S(1)}, f32[16,1024]{1,0:T(8,128)S(1)}, u32[]{:S(2)}, u32[]{:S(2)}) collective-permute-start(f32[16,1024]{1,0:T(8,128)S(1)} %bitcast.71), channel_id=1, source_target_pairs={{0,16},{16,0},{1,17},{17,1},{2,18},{18,2},{3,19},{19,3},{4,20},{20... | collective-permute-start | bytes 196616 | tf_op jit(solution)/shard_map/ppermute | solution.py:116
  117.9 4.4 %convert_bitcast_fusion.1 = bf16[1,1024,2048]{2,1,0:T(8,128)(2,1)} fusion(bf16[256,2048]{1,0:T(8,128)(2,1)S(1)} %copy-done.17, bf16[256,2048]{1,0:T(8,128)(2,1)S(1)} %copy-done.15, bf16[256,1024]{1,0:T(8,128)(2,1)S(1)} %collective-permute-done.9, bf16[256,1024]{1,0:T(8,128)(2,1)S(1)} %convolution_convert_fusion.2), kind=kOutput, calls=%fused_computation.13 | convolution fusion | flops 2155872256 | bytes 7340032 | tf_op jit(solution)/shard_map/dot_general | solution.py:26
  122.9 9.0 %all-to-all-done.1 = bf16[16,32,1024]{2,1,0:T(8,128)(2,1)S(1)} async-done(((bf16[16,32,1024]{2,1,0:T(8,128)(2,1)}), bf16[16,32,1024]{2,1,0:T(8,128)(2,1)S(1)}, u32[]{:S(2)}, u32[]{:S(2)}) %all-to-all-start.1) | async-done | bytes 1048608 | tf_op jit(solution)/shard_map/all_to_all | solution.py:133
  133.4 1.3 fusion.64
  (81 shorter events, 7.4 us)
Async XLA Ops:
  4.3 9.7 %collective-permute-start = (bf16[64,1024]{1,0:T(8,128)(2,1)}, bf16[64,1024]{1,0:T(8,128)(2,1)S(1)}, u32[]{:S(2)}, u32[]{:S(2)}) collective-permute-start(bf16[64,1024]{1,0:T(8,128)(2,1)} %get-tuple-element.25), channel_id=1, source_target_pairs={{0,2},{1,3},{2,0},{3,1},{4,6},{5,7},{6,4},{7,5},{8,10},{9,11},{10,... | collective-permute-start | bytes 393224 | tf_op jit(solution)/shard_map/ppermute | solution.py:124
  7.3 11.0 %collective-permute-start.1 = (bf16[64,1024]{1,0:T(8,128)(2,1)}, bf16[64,1024]{1,0:T(8,128)(2,1)S(1)}, u32[]{:S(2)}, u32[]{:S(2)}) collective-permute-start(bf16[64,1024]{1,0:T(8,128)(2,1)} %get-tuple-element.26), channel_id=1, source_target_pairs={{0,4},{1,5},{2,6},{3,7},{4,0},{5,1},{6,2},{7,3},{8,12},{9,13},{10,... | collective-permute-start | bytes 393224 | tf_op jit(solution)/shard_map/ppermute | solution.py:124
  8.9 10.1 %collective-permute-start.2 = (bf16[64,1024]{1,0:T(8,128)(2,1)}, bf16[64,1024]{1,0:T(8,128)(2,1)S(1)}, u32[]{:S(2)}, u32[]{:S(2)}) collective-permute-start(bf16[64,1024]{1,0:T(8,128)(2,1)} %get-tuple-element.27), channel_id=1, source_target_pairs={{0,6},{1,7},{2,4},{3,5},{4,2},{5,3},{6,0},{7,1},{8,14},{9,15},{10,... | collective-permute-start | bytes 393224 | tf_op jit(solution)/shard_map/ppermute | solution.py:124
  8.9 10.1 %collective-permute-start.3 = (bf16[64,1024]{1,0:T(8,128)(2,1)}, bf16[64,1024]{1,0:T(8,128)(2,1)S(1)}, u32[]{:S(2)}, u32[]{:S(2)}) collective-permute-start(bf16[64,1024]{1,0:T(8,128)(2,1)} %get-tuple-element.28), channel_id=1, source_target_pairs={{0,8},{1,9},{2,10},{3,11},{4,12},{5,13},{6,14},{7,15},{8,0},{9,1},... | collective-permute-start | bytes 393224 | tf_op jit(solution)/shard_map/ppermute | solution.py:124
  11.8 19.6 %collective-permute-start.4 = (bf16[64,1024]{1,0:T(8,128)(2,1)}, bf16[64,1024]{1,0:T(8,128)(2,1)S(1)}, u32[]{:S(2)}, u32[]{:S(2)}) collective-permute-start(bf16[64,1024]{1,0:T(8,128)(2,1)} %get-tuple-element.29), channel_id=1, source_target_pairs={{0,10},{1,11},{2,8},{3,9},{4,14},{5,15},{6,12},{7,13},{8,2},{9,3},... | collective-permute-start | bytes 393224 | tf_op jit(solution)/shard_map/ppermute | solution.py:124
  14.0 17.5 %collective-permute-start.5 = (bf16[64,1024]{1,0:T(8,128)(2,1)}, bf16[64,1024]{1,0:T(8,128)(2,1)S(1)}, u32[]{:S(2)}, u32[]{:S(2)}) collective-permute-start(bf16[64,1024]{1,0:T(8,128)(2,1)} %get-tuple-element.30), channel_id=1, source_target_pairs={{0,12},{1,13},{2,14},{3,15},{4,8},{5,9},{6,10},{7,11},{8,4},{9,5},... | collective-permute-start | bytes 393224 | tf_op jit(solution)/shard_map/ppermute | solution.py:124
  18.3 13.3 %collective-permute-start.6 = (bf16[64,1024]{1,0:T(8,128)(2,1)}, bf16[64,1024]{1,0:T(8,128)(2,1)S(1)}, u32[]{:S(2)}, u32[]{:S(2)}) collective-permute-start(bf16[64,1024]{1,0:T(8,128)(2,1)} %get-tuple-element.31), channel_id=1, source_target_pairs={{0,14},{1,15},{2,12},{3,13},{4,10},{5,11},{6,8},{7,9},{8,6},{9,7},... | collective-permute-start | bytes 393224 | tf_op jit(solution)/shard_map/ppermute | solution.py:124
  19.0 23.9 %copy-start.8 = (bf16[1024,16]{0,1:T(8,128)(2,1)S(1)}, bf16[1024,16]{0,1:T(8,128)(2,1)}, u32[]{:S(2)}) copy-start(bf16[1024,16]{0,1:T(8,128)(2,1)} %param.9) | copy-start | bytes 98308
  31.6 11.3 %collective-permute-start.7 = (bf16[256,1024]{1,0:T(8,128)(2,1)S(1)}, bf16[256,1024]{1,0:T(8,128)(2,1)S(1)}, u32[]{:S(2)}, u32[]{:S(2)}) collective-permute-start(bf16[256,1024]{1,0:T(8,128)(2,1)S(1)} %get-tuple-element.47), channel_id=1, source_target_pairs={{0,1},{1,0},{2,3},{3,2},{4,5},{5,4},{6,7},{7,6},{8,9},{9,8},{10,11... | collective-permute-start | bytes 1572872 | tf_op jit(solution)/shard_map/ppermute | solution.py:127
  34.7 8.3 %copy-start.5 = (bf16[256,512]{1,0:T(8,128)(2,1)S(1)}, bf16[256,512]{1,0:T(8,128)(2,1)}, u32[]{:S(2)}) copy-start(bf16[256,512]{1,0:T(8,128)(2,1)} %get-tuple-element.23) | copy-start | bytes 786436
  34.7 31.0 %all-to-all-start = ((bf16[16,32,1024]{2,1,0:T(8,128)(2,1)}), bf16[16,32,1024]{2,1,0:T(8,128)(2,1)S(1)}, u32[]{:S(2)}, u32[]{:S(2)}) async-start(bf16[16,32,1024]{2,1,0:T(8,128)(2,1)} %bitcast.68), calls=%async_computation | async-start | bytes 2097152 | tf_op jit(solution)/shard_map/all_to_all | solution.py:133
  43.4 14.3 %collective-permute-start.9 = (bf16[256,1024]{1,0:T(8,128)(2,1)S(1)}, bf16[256,1024]{1,0:T(8,128)(2,1)S(1)}, u32[]{:S(2)}, u32[]{:S(2)}) collective-permute-start(bf16[256,1024]{1,0:T(8,128)(2,1)S(1)} %convolution_convert_fusion.2), channel_id=1, source_target_pairs={{0,16},{16,0},{1,17},{17,1},{2,18},{18,2},{3,19},{19,3},{4,20},{20... | collective-permute-start | bytes 1572872 | tf_op jit(solution)/shard_map/ppermute | solution.py:116
  45.2 12.7 %copy-start.10 = (bf16[1,1024,2048]{2,1,0:T(8,128)(2,1)S(1)}, bf16[1,1024,2048]{2,1,0:T(8,128)(2,1)}, u32[]{:S(2)}) copy-start(bf16[1,1024,2048]{2,1,0:T(8,128)(2,1)} %param.10) | copy-start | bytes 12582916
  58.0 7.7 %copy-start.4 = (bf16[256,512]{1,0:T(8,128)(2,1)S(1)}, bf16[256,512]{1,0:T(8,128)(2,1)}, u32[]{:S(2)}) copy-start(bf16[256,512]{1,0:T(8,128)(2,1)} %get-tuple-element.32) | copy-start | bytes 786436
  65.7 2.7 %copy-start.13 = (f32[256,2048]{1,0:T(8,128)S(1)}, f32[256,2048]{1,0:T(8,128)}, u32[]{:S(2)}) copy-start(f32[256,2048]{1,0:T(8,128)} %fusion.6) | copy-start | bytes 6291460
  66.9 7.5 %copy-start.11 = (bf16[1,1024,2048]{2,1,0:T(8,128)(2,1)S(1)}, bf16[1,1024,2048]{2,1,0:T(8,128)(2,1)}, u32[]{:S(2)}) copy-start(bf16[1,1024,2048]{2,1,0:T(8,128)(2,1)} %param.10) | copy-start | bytes 12582916
  66.9 14.5 %collective-permute-start.8 = (bf16[256,1024]{1,0:T(8,128)(2,1)S(1)}, bf16[256,1024]{1,0:T(8,128)(2,1)S(1)}, u32[]{:S(2)}, u32[]{:S(2)}) collective-permute-start(bf16[256,1024]{1,0:T(8,128)(2,1)S(1)} %get-tuple-element.65), channel_id=1, source_target_pairs={{0,16},{16,0},{1,17},{17,1},{2,18},{18,2},{3,19},{19,3},{4,20},{20... | collective-permute-start | bytes 1572872 | tf_op jit(solution)/shard_map/ppermute | solution.py:116
  74.2 1.5 %copy-start.14 = (bf16[256,2048]{1,0:T(8,128)(2,1)}, bf16[256,2048]{1,0:T(8,128)(2,1)S(1)}, u32[]{:S(2)}) copy-start(bf16[256,2048]{1,0:T(8,128)(2,1)S(1)} %get-tuple-element.46) | copy-start | bytes 3145732
  74.4 7.1 %copy-start.9 = (bf16[1,2048,1024]{2,1,0:T(8,128)(2,1)S(1)}, bf16[1,2048,1024]{2,1,0:T(8,128)(2,1)}, u32[]{:S(2)}) copy-start(bf16[1,2048,1024]{2,1,0:T(8,128)(2,1)} %param.11) | copy-start | bytes 12582916
  74.4 7.0 %copy-start.12 = (f32[256,2048]{1,0:T(8,128)S(1)}, f32[256,2048]{1,0:T(8,128)}, u32[]{:S(2)}) copy-start(f32[256,2048]{1,0:T(8,128)} %fusion.2) | copy-start | bytes 6291460
  85.3 2.1 %copy-start.16 = (bf16[256,2048]{1,0:T(8,128)(2,1)}, bf16[256,2048]{1,0:T(8,128)(2,1)S(1)}, u32[]{:S(2)}) copy-start(bf16[256,2048]{1,0:T(8,128)(2,1)S(1)} %get-tuple-element.45) | copy-start | bytes 3145732
  87.4 14.0 %copy-start.3 = (bf16[512,256]{1,0:T(8,128)(2,1)S(1)}, bf16[512,256]{1,0:T(8,128)(2,1)}, u32[]{:S(2)}) copy-start(bf16[512,256]{1,0:T(8,128)(2,1)} %get-tuple-element.22) | copy-start | bytes 786436
  87.4 13.9 %collective-permute-start.10 = (bf16[256,1024]{1,0:T(8,128)(2,1)}, bf16[256,1024]{1,0:T(8,128)(2,1)S(1)}, u32[]{:S(2)}, u32[]{:S(2)}) collective-permute-start(bf16[256,1024]{1,0:T(8,128)(2,1)} %fusion.38), channel_id=1, source_target_pairs={{0,16},{16,0},{1,17},{17,1},{2,18},{18,2},{3,19},{19,3},{4,20},{20... | collective-permute-start | bytes 1572872 | tf_op jit(solution)/shard_map/ppermute | solution.py:116
  89.8 13.4 %all-to-all-start.2 = ((f32[16,1,1024]{2,1,0:T(1,128)}), f32[16,1,1024]{2,1,0:T(1,128)S(1)}, u32[]{:S(2)}, u32[]{:S(2)}) async-start(f32[16,1,1024]{2,1,0:T(1,128)} %broadcast_in_dim.15), calls=%async_computation.2 | async-start | bytes 131072 | tf_op jit(solution)/shard_map/all_to_all | solution.py:202
  101.5 7.6 %copy-start = (bf16[256,1024]{1,0:T(8,128)(2,1)S(1)}, bf16[256,1024]{1,0:T(8,128)(2,1)}, u32[]{:S(2)}) copy-start(bf16[256,1024]{1,0:T(8,128)(2,1)} %tokens_ref.1) | copy-start | bytes 1572868
  101.5 8.1 %copy-start.7 = (bf16[1,2,1024]{2,1,0:T(2,128)(2,1)S(1)}, bf16[1,2,1024]{2,1,0:T(2,128)(2,1)}, u32[]{:S(2)}) copy-start(bf16[1,2,1024]{2,1,0:T(2,128)(2,1)} %param.8) | copy-start | bytes 12292
  103.2 28.8 %all-to-all-start.1 = ((bf16[16,32,1024]{2,1,0:T(8,128)(2,1)}), bf16[16,32,1024]{2,1,0:T(8,128)(2,1)S(1)}, u32[]{:S(2)}, u32[]{:S(2)}) async-start(bf16[16,32,1024]{2,1,0:T(8,128)(2,1)} %bitcast.8), calls=%async_computation.1 | async-start | bytes 2097152 | tf_op jit(solution)/shard_map/all_to_all | solution.py:133
  110.5 7.4 %copy-start.15 = (bf16[256,2048]{1,0:T(8,128)(2,1)S(1)}, bf16[256,2048]{1,0:T(8,128)(2,1)}, u32[]{:S(2)}) copy-start(bf16[256,2048]{1,0:T(8,128)(2,1)} %copy-done.14) | copy-start | bytes 3145732
  110.5 7.4 %copy-start.17 = (bf16[256,2048]{1,0:T(8,128)(2,1)S(1)}, bf16[256,2048]{1,0:T(8,128)(2,1)}, u32[]{:S(2)}) copy-start(bf16[256,2048]{1,0:T(8,128)(2,1)} %copy-done.16) | copy-start | bytes 3145732
  116.3 15.7 %copy-start.6 = (bf16[512,256]{1,0:T(8,128)(2,1)S(1)}, bf16[512,256]{1,0:T(8,128)(2,1)}, u32[]{:S(2)}) copy-start(bf16[512,256]{1,0:T(8,128)(2,1)} %get-tuple-element.21.select_ref) | copy-start | bytes 786436
  116.3 6.0 %collective-permute-start.11 = (f32[16,1024]{1,0:T(8,128)S(1)}, f32[16,1024]{1,0:T(8,128)S(1)}, u32[]{:S(2)}, u32[]{:S(2)}) collective-permute-start(f32[16,1024]{1,0:T(8,128)S(1)} %bitcast.71), channel_id=1, source_target_pairs={{0,16},{16,0},{1,17},{17,1},{2,18},{18,2},{3,19},{19,3},{4,20},{20... | collective-permute-start | bytes 196616 | tf_op jit(solution)/shard_map/ppermute | solution.py:116
  122.9 10.4 %copy-start.1 = (bf16[256,1024]{1,0:T(8,128)(2,1)S(1)}, bf16[256,1024]{1,0:T(8,128)(2,1)}, u32[]{:S(2)}) copy-start(bf16[256,1024]{1,0:T(8,128)(2,1)} %grad_ref.1) | copy-start | bytes 1572868
  (2 other events, 2.4 us)
